TPU v7x, 256 devices: a whole 4x4x8 slice. The times are simulated.
256 devices in a mesh: dp: 32 (over x, y, core), mp: 8 (over z).
Axes of the slice: x: 4, y: 4, z: 8, core: 2. Of those that a mesh axis runs over, the one named last changes fastest.
Arguments:
- queries: bfloat16 [4096, 64, 128], P('dp', 'mp'), may hold values from -6 to 6
- key_cache: bfloat16 [4096, 8, 128, 128], P('dp', 'mp'), may hold values from -6 to 6
- value_cache: bfloat16 [4096, 8, 128, 128], P('dp', 'mp'), may hold values from -6 to 6
- key_new: bfloat16 [4096, 8, 128], P('dp', 'mp'), may hold values from -6 to 6
- value_new: bfloat16 [4096, 8, 128], P('dp', 'mp'), may hold values from -6 to 6
- lengths: int32 [4096], P('dp'), may hold values from 1 to 128, as said below
- occupied: int32 [4096], P('dp'), may hold values 0 or 1
- slot_request: int32 [4096], P('dp'), may hold values from 0 to 4095, as said below
- request_adapter: int32 [4096], replicated, may hold values from 0 to 63, as said below
- out_weight: bfloat16 [8192, 4096], P('mp'), may hold values from -0.375 to 0.375
- shrink_weight: bfloat16 [64, 8192, 64], P('dp', 'mp'), may hold values from -0.375 to 0.375
- expand_weight: bfloat16 [64, 64, 4096], P('dp', None, 'mp'), may hold values from -0.75 to 0.75
Outputs:
- mixed: bfloat16 [4096, 4096], P('dp', 'mp')
Inputs may be any that keep to these rules, and one draw needn't show every extreme that they name: `slot_request`: A permutation: each request stands in exactly one slot. `request_adapter`: adapter n is owned by dp index n // 2. Among the slots of one dp index, at most 8 hold requests whose adapters one dp index owns; in every draw some dp index owns the adapters of exactly 8 slots of every dp index. `lengths`: each dp index has a slot of length 128.
All inputs are finite; a program needn't handle non-finite values. No bound on the sum of `occupied` on one device may be relied on, other than what follows from the above.
Results may differ from a plain program's by a relative error of at most 0.011.
Values may be sent and summed in bfloat16 or wider, within the bound.
A program may use at most 64 MiB of HBM per device.

v0:
```python
import math
import jax
import jax.numpy as jnp
from jax import lax
from jax.sharding import PartitionSpec as P


def attend(queries, key_cache, value_cache, key_new, value_new, lengths):
    rows, heads, width = queries.shape
    kv_local = key_cache.shape[1]
    group = heads // kv_local
    inverse = 1.0 / math.sqrt(width)
    grouped = queries.reshape(rows, kv_local, group, width)
    cached = (
        jnp.einsum("bgjd,bgtd->bgjt", grouped, key_cache, preferred_element_type=jnp.float32)
        * inverse
    )
    fresh = (
        jnp.einsum("bgjd,bgd->bgj", grouped, key_new, preferred_element_type=jnp.float32) * inverse
    )
    valid = jnp.arange(key_cache.shape[2])[None, :] < lengths[:, None]
    cached = jnp.where(valid[:, None, None, :], cached, -jnp.inf)
    top = jnp.maximum(jnp.max(cached, axis=-1), fresh)
    cached_exp = jnp.exp(cached - top[..., None])
    fresh_exp = jnp.exp(fresh - top)
    total = jnp.sum(cached_exp, axis=-1) + fresh_exp
    cached_w = (cached_exp / total[..., None]).astype(jnp.bfloat16)
    fresh_w = (fresh_exp / total).astype(jnp.bfloat16)
    summed = jnp.einsum(
        "bgjt,bgtd->bgjd", cached_w, value_cache, preferred_element_type=jnp.float32
    )
    summed = (
        summed
        + fresh_w.astype(jnp.float32)[..., None] * value_new.astype(jnp.float32)[:, :, None, :]
    )
    return summed.reshape(rows, heads * width).astype(jnp.bfloat16)


def body(
    queries,
    key_cache,
    value_cache,
    key_new,
    value_new,
    lengths,
    occupied,
    slot_request,
    request_adapter,
    out_weight,
    shrink_weight,
    expand_weight,
):
    rows = queries.shape[0]
    attended = attend(queries, key_cache, value_cache, key_new, value_new, lengths)
    owners_count = lax.axis_size("dp")
    adapters_here = shrink_weight.shape[0]
    rank_width = shrink_weight.shape[2]
    out_local = expand_weight.shape[2]
    capacity = 2 * rows // owners_count
    matches = (
        slot_request[:, None] == jnp.arange(request_adapter.shape[0], dtype=jnp.int32)[None, :]
    )
    slot_adapter = jnp.sum(jnp.where(matches, request_adapter[None, :], 0), axis=1)
    owner = slot_adapter // adapters_here
    local_ids = slot_adapter % adapters_here
    owner_onehot = (owner[:, None] == jnp.arange(owners_count, dtype=jnp.int32)[None, :]).astype(
        jnp.int32
    )
    earlier = jnp.cumsum(owner_onehot, axis=0) - owner_onehot
    position = jnp.sum(earlier * owner_onehot, axis=1)
    slot_code = owner * capacity + position
    dispatch = jnp.arange(owners_count * capacity, dtype=jnp.int32)[:, None] == slot_code[None, :]
    send_rows = jnp.dot(
        dispatch.astype(jnp.bfloat16), attended, preferred_element_type=jnp.float32
    ).astype(jnp.bfloat16)
    send_rows = send_rows.reshape(owners_count, capacity, attended.shape[1])
    send_ids = jnp.sum(jnp.where(dispatch, (local_ids + 1)[None, :], 0), axis=1).reshape(
        owners_count, capacity
    )
    combine = (
        slot_code[:, None] == jnp.arange(owners_count * capacity, dtype=jnp.int32)[None, :]
    ).astype(jnp.bfloat16)
    partial_value = jnp.dot(attended, out_weight, preferred_element_type=jnp.float32)
    full = lax.psum(partial_value, "mp")
    base = lax.dynamic_slice_in_dim(full, lax.axis_index("mp") * out_local, out_local, 1)
    got_rows = lax.all_to_all(send_rows, "dp", split_axis=0, concat_axis=0, tiled=True)
    got_ids = lax.all_to_all(send_ids, "dp", split_axis=0, concat_axis=0, tiled=True)
    flat = got_rows.reshape(owners_count * capacity, got_rows.shape[2])
    wanted = got_ids.reshape(owners_count * capacity) - 1
    partial_value = jnp.einsum(
        "md,adr->mar", flat, shrink_weight, preferred_element_type=jnp.float32
    )
    which = jnp.arange(adapters_here, dtype=jnp.int32)[None, :] == wanted[:, None]
    partial_value = jnp.where(which[:, :, None], partial_value, 0.0)
    summed = lax.psum(
        partial_value.reshape(owners_count * capacity, adapters_here * rank_width), "mp"
    )
    low = summed.astype(jnp.bfloat16).reshape(owners_count * capacity, adapters_here, rank_width)
    delta = 0.5 * jnp.einsum("mar,are->me", low, expand_weight, preferred_element_type=jnp.float32)
    delta = delta.astype(jnp.bfloat16).reshape(owners_count, capacity, out_local)
    back = lax.all_to_all(delta, "dp", split_axis=0, concat_axis=0, tiled=True)
    correction = jnp.dot(
        combine,
        back.reshape(owners_count * capacity, out_local),
        preferred_element_type=jnp.float32,
    )
    return (occupied.astype(jnp.float32)[:, None] * (base + correction)).astype(jnp.bfloat16)


def solution(mesh):
    placed = (
        P("dp", "mp", None),
        P("dp", "mp", None, None),
        P("dp", "mp", None, None),
        P("dp", "mp", None),
        P("dp", "mp", None),
        P("dp"),
        P("dp"),
        P("dp"),
        P(),
        P("mp", None),
        P("dp", "mp", None),
        P("dp", None, "mp"),
    )
    return jax.shard_map(body, mesh=mesh, in_specs=placed, out_specs=P("dp", "mp"), check_vma=False)
```

profile of v0, /device:TPU:22, one launch (start us, length us, event | category | flops | bytes accessed | tf_op | source)
XLA Modules:
  0.0 117.1 jit_solution(17132844115245272164)
XLA Ops:
  6.5 0.0 copy-start
  6.5 0.0 copy-start.1
  6.5 0.0 copy-start.6
  6.5 0.0 copy-start.3
  6.5 0.0 all-reduce.3.cloned.1.call-start
  6.6 0.8 iota_compare_fusion.6
  7.4 4.6 %fusion.42 = (f32[128,8]{1,0:T(8,128)S(1)}, f32[128,8,128]{2,1,0:T(8,128)S(1)}) fusion(bf16[128,8,128]{2,1,0:T(8,128)(2,1)} %param.12, bf16[128,1,128,128]{3,2,1,0:T(8,128)(2,1)} %param.13, pred[128,128]{1,0:T(8,128)(4,1)S(1)} %iota_compare_fusion.6), kind=kOutput, calls=%fused_computation.60 | convolution fusion | flops 33946624 | bytes 5001216 | tf_op jit(solution)/shard_map/bgjd,bgtd->bgjt/dot_general | solution.py:15
  12.0 0.1 copy.19
  12.1 0.0 copy-done.1
  12.1 0.0 copy-done.6
  12.1 0.3 fusion.36
  12.4 0.1 copy.20
  12.6 0.4 fusion.24
  13.0 0.1 copy.22
  13.1 0.1 copy.23
  13.2 0.0 copy-done.3
  13.3 3.5 %fusion.16 = bf16[128,8,128]{2,1,0:T(8,128)(2,1)S(1)} fusion(bf16[128,1,128,128]{3,2,1,0:T(8,128)(2,1)} %param.14, f32[128,8,128]{2,1,0:T(8,128)S(1)} %get-tuple-element.10, f32[128,128]{1,0:T(8,128)S(1)} %bitcast_convert_fusion, f32[128,8]{1,0:T(8,128)S(1)} %copy.23, f32[128,8]{1,0:T(8,128)S(1)} %copy.22, f32[128,8]{1,0:T(8,128)S(1)} %copy.20), kind=kOutput, calls=%fused_computation.14 | convolution fusion | flops 34340864 | bytes 5058560 | tf_op jit(solution)/shard_map/bgjt,bgtd->bgjd/dot_general | solution.py:29
  16.7 0.0 copy-start.4
  16.7 0.0 copy-start.5
  16.7 6.0 %fusion.26 = f32[128,4096]{1,0:T(8,128)} fusion(bf16[1024,4096]{1,0:T(8,128)(2,1)} %param.21, bf16[16,8,8,128]{3,2,1,0:T(8,128)(2,1)S(1)} %bitcast.75), kind=kOutput, calls=%fused_computation.25 | convolution fusion | flops 1073741824 | bytes 10747904 | tf_op jit(solution)/shard_map/dot_general | solution.py:83
  22.7 0.0 copy-start.2
  22.7 0.0 copy-start.7
  22.7 0.0 all-reduce.3.cloned.1.call-update
  22.7 0.0 copy-done.4
  22.8 0.0 copy-done.5
  22.8 0.4 select_reduce_fusion
  23.2 0.1 fusion.35
  23.3 0.2 reduce_window_sum.11
  23.5 0.2 select_reduce_fusion.2
  23.7 0.1 select_reduce_fusion.1
  23.8 0.7 all_to_all.12
  24.5 7.4 %all-to-all-start = ((s32[32,1,8]{2,1,0:T(1,128)}), s32[32,1,8]{2,1,0:T(1,128)S(1)}, u32[]{:S(2)}, u32[]{:S(2)}) async-start(s32[32,1,8]{2,1,0:T(1,128)} %bitcast.6), calls=%async_computation | async-start | bytes 32768 | tf_op jit(solution)/shard_map/all_to_all | solution.py:87
  31.9 1.1 fusion.4
  33.0 2.5 %all-to-all-done = s32[32,1,8]{2,1,0:T(1,128)S(1)} async-done(((s32[32,1,8]{2,1,0:T(1,128)}), s32[32,1,8]{2,1,0:T(1,128)S(1)}, u32[]{:S(2)}, u32[]{:S(2)}) %all-to-all-start) | async-done | bytes 1056 | tf_op jit(solution)/shard_map/all_to_all | solution.py:87
  35.4 7.6 %all-to-all-start.1 = ((bf16[32,8,1024]{2,1,0:T(8,128)(2,1)}), bf16[32,8,1024]{2,1,0:T(8,128)(2,1)S(1)}, u32[]{:S(2)}, u32[]{:S(2)}) async-start(bf16[32,8,1024]{2,1,0:T(8,128)(2,1)} %fusion.4), calls=%async_computation.1 | async-start | bytes 1048576 | tf_op jit(solution)/shard_map/all_to_all | solution.py:86
  43.1 0.1 sub.34
  43.2 7.9 %all-to-all-done.1 = bf16[32,8,1024]{2,1,0:T(8,128)(2,1)S(1)} async-done(((bf16[32,8,1024]{2,1,0:T(8,128)(2,1)}), bf16[32,8,1024]{2,1,0:T(8,128)(2,1)S(1)}, u32[]{:S(2)}, u32[]{:S(2)}) %all-to-all-start.1) | async-done | bytes 524320 | tf_op jit(solution)/shard_map/all_to_all | solution.py:86
  51.1 0.0 copy-done
  51.1 0.3 fusion.22
  51.5 34.2 %all-reduce.4 = bf16[256,128]{0,1:T(8,128)(2,1)S(1)} all-reduce(f32[256,128]{0,1:T(8,128)S(1)} %bitcast.78), channel_id=1, replica_groups=mesh['dp'=32,'mp'=8] {'mp'}, use_global_device_ids=true, to_apply=%region_7.8 | all-reduce | flops 32768 | bytes 196608 | tf_op jit(solution)/shard_map/psum | solution.py:95
  85.7 0.0 copy-done.2
  85.7 0.9 fusion.19
  86.6 7.1 %all-to-all-start.2 = ((bf16[32,8,512]{2,1,0:T(8,128)(2,1)}), bf16[32,8,512]{2,1,0:T(8,128)(2,1)S(1)}, u32[]{:S(2)}, u32[]{:S(2)}) async-start(bf16[32,8,512]{2,1,0:T(8,128)(2,1)} %fusion.19), calls=%async_computation.2 | async-start | bytes 524288 | tf_op jit(solution)/shard_map/all_to_all | solution.py:101
  93.8 0.0 copy-done.7
  93.8 5.3 %all-to-all-done.2 = bf16[32,8,512]{2,1,0:T(8,128)(2,1)S(1)} async-done(((bf16[32,8,512]{2,1,0:T(8,128)(2,1)}), bf16[32,8,512]{2,1,0:T(8,128)(2,1)S(1)}, u32[]{:S(2)}, u32[]{:S(2)}) %all-to-all-start.2) | async-done | bytes 262176 | tf_op jit(solution)/shard_map/all_to_all | solution.py:101
  99.1 9.4 %all-reduce.3.cloned.1.call-done = f32[128,4096]{1,0:T(8,128)} async-done(((f32[128,4096]{1,0:T(8,128)}), f32[128,4096]{1,0:T(8,128)}) %all-reduce.3.cloned.1.call-update) | async-done | bytes 2097168 | tf_op jit(solution)/shard_map/psum | solution.py:84
  108.5 1.8 %fusion.21 = bf16[128,512]{1,0:T(8,128)(2,1)} fusion(bf16[32,8,512]{2,1,0:T(8,128)(2,1)S(1)} %all-to-all-done.2, f32[128,4096]{1,0:T(8,128)} %all-reduce.3.cloned.1.call-done, s32[]{:T(128)S(6)} %select_n.48, f32[128]{0:T(128)S(1)} %convert_element_type.39, s32[128]{0:T(128)S(1)} %multiply_add_fusion), kind=kOutput, calls=%fused_computation.18 | convolution fusion | flops 33783808 | bytes 656388 | tf_op jit(solution)/shard_map/dot_general | solution.py:102
  (11 shorter events, 0.2 us)
Async XLA Ops:
  6.5 44.6 %copy-start = (bf16[2,1024,64]{1,2,0:T(8,128)(2,1)S(1)}, bf16[2,1024,64]{1,2,0:T(8,128)(2,1)}, u32[]{:S(2)}) copy-start(bf16[2,1024,64]{1,2,0:T(8,128)(2,1)} %param.22) | copy-start | bytes 786436
  6.5 5.5 %copy-start.1 = (bf16[128,8,128]{2,1,0:T(8,128)(2,1)S(1)}, bf16[128,8,128]{2,1,0:T(8,128)(2,1)}, u32[]{:S(2)}) copy-start(bf16[128,8,128]{2,1,0:T(8,128)(2,1)} %param.12) | copy-start | bytes 786436
  6.5 5.5 %copy-start.6 = (bf16[128,1,128]{2,0,1:T(8,128)(2,1)S(1)}, bf16[128,1,128]{2,0,1:T(8,128)(2,1)}, u32[]{:S(2)}) copy-start(bf16[128,1,128]{2,0,1:T(8,128)(2,1)} %param.15) | copy-start | bytes 98308
  6.5 6.7 %copy-start.3 = (bf16[128,1,128]{2,0,1:T(8,128)(2,1)S(1)}, bf16[128,1,128]{2,0,1:T(8,128)(2,1)}, u32[]{:S(2)}) copy-start(bf16[128,1,128]{2,0,1:T(8,128)(2,1)} %param.16) | copy-start | bytes 98308
  6.5 101.9 %all-reduce.3.cloned.1.call-start = ((), (), s32[]{:S(2)}) async-start(), calls=%async_computation.3 | async-start | bytes 4194304 | tf_op jit(solution)/shard_map/psum | solution.py:84
  16.7 6.0 %copy-start.4 = (s32[4096]{0:T(1024)S(1)}, s32[4096]{0:T(1024)}, u32[]{:S(2)}) copy-start(s32[4096]{0:T(1024)} %param.20) | copy-start | bytes 49156
  16.7 6.0 %copy-start.5 = (s32[128]{0:T(128)S(1)}, s32[128]{0:T(128)}, u32[]{:S(2)}) copy-start(s32[128]{0:T(128)} %param.19) | copy-start | bytes 1540
  22.7 63.0 %copy-start.2 = (bf16[2,64,512]{2,1,0:T(8,128)(2,1)S(1)}, bf16[2,64,512]{2,1,0:T(8,128)(2,1)}, u32[]{:S(2)}) copy-start(bf16[2,64,512]{2,1,0:T(8,128)(2,1)} %param.23) | copy-start | bytes 393220
  22.7 71.1 %copy-start.7 = (s32[128]{0:T(128)S(1)}, s32[128]{0:T(128)}, u32[]{:S(2)}) copy-start(s32[128]{0:T(128)} %param.18) | copy-start | bytes 1540
  24.5 11.0 %all-to-all-start = ((s32[32,1,8]{2,1,0:T(1,128)}), s32[32,1,8]{2,1,0:T(1,128)S(1)}, u32[]{:S(2)}, u32[]{:S(2)}) async-start(s32[32,1,8]{2,1,0:T(1,128)} %bitcast.6), calls=%async_computation | async-start | bytes 32768 | tf_op jit(solution)/shard_map/all_to_all | solution.py:87
  35.4 15.7 %all-to-all-start.1 = ((bf16[32,8,1024]{2,1,0:T(8,128)(2,1)}), bf16[32,8,1024]{2,1,0:T(8,128)(2,1)S(1)}, u32[]{:S(2)}, u32[]{:S(2)}) async-start(bf16[32,8,1024]{2,1,0:T(8,128)(2,1)} %fusion.4), calls=%async_computation.1 | async-start | bytes 1048576 | tf_op jit(solution)/shard_map/all_to_all | solution.py:86
  86.6 12.4 %all-to-all-start.2 = ((bf16[32,8,512]{2,1,0:T(8,128)(2,1)}), bf16[32,8,512]{2,1,0:T(8,128)(2,1)S(1)}, u32[]{:S(2)}, u32[]{:S(2)}) async-start(bf16[32,8,512]{2,1,0:T(8,128)(2,1)} %fusion.19), calls=%async_computation.2 | async-start | bytes 524288 | tf_op jit(solution)/shard_map/all_to_all | solution.py:101
Sparse Core Ops, SparseCore 0:
  22.9 85.5 all-reduce.2
where the time goes:
time: 118 us; the launch traced here: 117 us
  blocking collectives  34.2 us (29%)
  waiting for transfers between devices  25.1 us (21%)
  starting transfers between devices  22.2 us (19%)
  matrix products  18.5 us (16%)
  between operations  13.6 us (12%)
  other arithmetic  2.26 us (2%)
  local copies, waits for them, and re-layouts  1.31 us (1%)
    psum x1, blocking collectives, body(): lax.psum(partial_value.reshape(owners_count * capacity, adapters_here * r...  34.2 us
    psum x1, waiting for transfers between devices, body(): full = lax.psum(partial_value, 'mp')  9.39 us
    all_to_all x1, waiting for transfers between devices, body(): lax.all_to_all(send_rows, 'dp', split_axis=0, concat_axis=0, tiled=True)  7.91 us
    all_to_all x1, starting transfers between devices, body(): lax.all_to_all(send_rows, 'dp', split_axis=0, concat_axis=0, tiled=True)  7.63 us
    all_to_all x1, starting transfers between devices, body(): lax.all_to_all(send_ids, 'dp', split_axis=0, concat_axis=0, tiled=True)  7.41 us
    all_to_all x1, starting transfers between devices, body(): back = lax.all_to_all(delta, 'dp', split_axis=0, concat_axis=0, tiled=True)  7.14 us
    dot_general x1, matrix products, body(): jnp.dot(attended, out_weight, preferred_element_type=jnp.float32)  5.97 us
    all_to_all x1, waiting for transfers between devices, body(): back = lax.all_to_all(delta, 'dp', split_axis=0, concat_axis=0, tiled=True)  5.27 us
  transfers between devices with their start and end apart: 4, of which 4 were waited for; matrix products, arithmetic and copies ran while one was open for 3% of the time, Pallas kernels for 0%

commit v1 on v0

--- a/solution.py
+++ b/solution.py
@@ -81,7 +81,9 @@
         slot_code[:, None] == jnp.arange(owners_count * capacity, dtype=jnp.int32)[None, :]
     ).astype(jnp.bfloat16)
     partial_value = jnp.dot(attended, out_weight, preferred_element_type=jnp.float32)
-    full = lax.psum(partial_value, "mp")
+    full = partial_value
+    for hop in (1, 2, 4):
+        full = full + lax.ppermute(full, "mp", [(dev, dev ^ hop) for dev in range(8)])
     base = lax.dynamic_slice_in_dim(full, lax.axis_index("mp") * out_local, out_local, 1)
     got_rows = lax.all_to_all(send_rows, "dp", split_axis=0, concat_axis=0, tiled=True)
     got_ids = lax.all_to_all(send_ids, "dp", split_axis=0, concat_axis=0, tiled=True)

time: 118 us -> 298 us (2.53); the launches traced: 117 us -> 293 us
  waiting for transfers between devices: 25.1 us -> 151 us
  blocking collectives: 34.2 us -> 84.8 us
  between operations: 13.6 us -> 0.22 us
  starting transfers between devices: 22.2 us -> 34.1 us
    ppermute x0 -> x3, waiting for transfers between devices: none -> 135 us  [body(): lax.ppermute(full, 'mp', [(dev, dev ^ hop) for dev in range(8)])]
    psum x1, blocking collectives: 34.2 us -> 84.8 us  [body(): lax.psum(partial_value.reshape(owners_count * capacity, adapters_here * r...]
    ppermute x0 -> x3, starting transfers between devices: none -> 11.6 us  [body(): lax.ppermute(full, 'mp', [(dev, dev ^ hop) for dev in range(8)])]
    psum x1 -> x0, waiting for transfers between devices: 9.39 us -> none  [body(): full = lax.psum(partial_value, 'mp')]
  transfers between devices with their start and end apart: 4 -> 6, of which waited for: 4 -> 5; matrix products, arithmetic and copies ran while one was open for 3% -> 1% of each run, Pallas kernels for 0% -> 0%
where the time goes in v1:
time: 298 us; the launch traced here: 293 us
  waiting for transfers between devices  151 us (51%)
  blocking collectives  84.8 us (28%)
  starting transfers between devices  34.1 us (11%)
  matrix products  18.2 us (6%)
  other arithmetic  3.59 us (1%)
    ppermute x3, waiting for transfers between devices, body(): lax.ppermute(full, 'mp', [(dev, dev ^ hop) for dev in range(8)])  135 us
    psum x1, blocking collectives, body(): lax.psum(partial_value.reshape(owners_count * capacity, adapters_here * r...  84.8 us
    ppermute x3, starting transfers between devices, body(): lax.ppermute(full, 'mp', [(dev, dev ^ hop) for dev in range(8)])  11.6 us
    all_to_all x1, waiting for transfers between devices, body(): lax.all_to_all(send_rows, 'dp', split_axis=0, concat_axis=0, tiled=True)  7.91 us
    all_to_all x1, starting transfers between devices, body(): lax.all_to_all(send_rows, 'dp', split_axis=0, concat_axis=0, tiled=True)  7.62 us
    all_to_all x1, starting transfers between devices, body(): lax.all_to_all(send_ids, 'dp', split_axis=0, concat_axis=0, tiled=True)  7.4 us
    all_to_all x1, starting transfers between devices, body(): back = lax.all_to_all(delta, 'dp', split_axis=0, concat_axis=0, tiled=True)  7.4 us
  transfers between devices with their start and end apart: 6, of which 5 were waited for; matrix products, arithmetic and copies ran while one was open for 1% of the time, Pallas kernels for 0%

profile of v1, /device:TPU:22, one launch (start us, length us, event | category | flops | bytes accessed | tf_op | source)
XLA Modules:
  0.0 292.9 jit_solution(11947067583230288643)
XLA Ops:
  0.0 0.0 copy-start
  0.0 0.8 iota_compare_fusion.6
  0.8 1.2 fusion.40
  2.1 0.8 bitcast_convert_fusion
  2.9 4.6 %fusion.46 = (f32[128,8]{1,0:T(8,128)S(1)}, f32[128,8,128]{2,1,0:T(8,128)S(1)}) fusion(bf16[128,8,128]{2,1,0:T(8,128)(2,1)} %param.12, bf16[128,1,128,128]{3,2,1,0:T(8,128)(2,1)} %param.13, pred[128,128]{1,0:T(8,128)(4,1)S(1)} %iota_compare_fusion.6), kind=kOutput, calls=%fused_computation.62 | convolution fusion | flops 33946624 | bytes 5001216 | tf_op jit(solution)/shard_map/bgjd,bgtd->bgjt/dot_general | solution.py:15
  7.5 0.1 copy.19
  7.6 0.1 copy.20
  7.7 0.4 fusion.22
  8.1 0.1 copy.22
  8.3 0.1 copy.23
  8.4 3.5 %fusion.16 = bf16[128,8,128]{2,1,0:T(8,128)(2,1)S(1)} fusion(bf16[128,1,128,128]{3,2,1,0:T(8,128)(2,1)} %param.14, f32[128,8,128]{2,1,0:T(8,128)S(1)} %get-tuple-element.10, f32[128,128]{1,0:T(8,128)S(1)} %bitcast_convert_fusion, f32[128,8]{1,0:T(8,128)S(1)} %copy.23, f32[128,8]{1,0:T(8,128)S(1)} %copy.22, f32[128,8]{1,0:T(8,128)S(1)} %copy.20), kind=kOutput, calls=%fused_computation.14 | convolution fusion | flops 34340864 | bytes 5058560 | tf_op jit(solution)/shard_map/bgjt,bgtd->bgjd/dot_general | solution.py:29
  11.8 4.6 %fusion.24 = f32[128,4096]{1,0:T(8,128)S(1)} fusion(bf16[1024,4096]{1,0:T(8,128)(2,1)} %param.21, bf16[16,8,8,128]{3,2,1,0:T(8,128)(2,1)S(1)} %bitcast.77), kind=kOutput, calls=%fused_computation.22 | convolution fusion | flops 1073741824 | bytes 10747904 | tf_op jit(solution)/shard_map/dot_general | solution.py:83
  16.5 0.0 copy-start.2
  16.5 0.0 copy-start.3
  16.5 2.0 collective-permute-start
  18.5 45.6 %collective-permute-done = f32[128,4096]{1,0:T(8,128)S(1)} collective-permute-done((f32[128,4096]{1,0:T(8,128)S(1)}, f32[128,4096]{1,0:T(8,128)S(1)}, u32[]{:S(2)}, u32[]{:S(2)}) %collective-permute-start) | collective-permute-done | bytes 2097184 | tf_op jit(solution)/shard_map/ppermute | solution.py:86
  64.1 0.3 add.74
  64.5 3.4 %collective-permute-start.1 = (f32[128,4096]{1,0:T(8,128)S(1)}, f32[128,4096]{1,0:T(8,128)S(1)}, u32[]{:S(2)}, u32[]{:S(2)}) collective-permute-start(f32[128,4096]{1,0:T(8,128)S(1)} %add.74), channel_id=1, source_target_pairs={{0,2},{1,3},{2,0},{3,1},{4,6},{5,7},{6,4},{7,5},{8,10},{9,11},{10,... | collective-permute-start | bytes 6291464 | tf_op jit(solution)/shard_map/ppermute | solution.py:86
  67.8 0.0 copy-done.2
  67.8 0.0 copy-done.3
  67.8 0.4 select_reduce_fusion
  68.3 89.5 %collective-permute-done.1 = f32[128,4096]{1,0:T(8,128)S(1)} collective-permute-done((f32[128,4096]{1,0:T(8,128)S(1)}, f32[128,4096]{1,0:T(8,128)S(1)}, u32[]{:S(2)}, u32[]{:S(2)}) %collective-permute-start.1) | collective-permute-done | bytes 2097184 | tf_op jit(solution)/shard_map/ppermute | solution.py:86
  157.7 0.2 add.75
  158.0 0.0 copy-start.1
  158.0 6.3 %collective-permute-start.2 = (f32[128,4096]{1,0:T(8,128)S(1)}, f32[128,4096]{1,0:T(8,128)}, u32[]{:S(2)}, u32[]{:S(2)}) collective-permute-start(f32[128,4096]{1,0:T(8,128)S(1)} %add.75), channel_id=1, source_target_pairs={{0,4},{1,5},{2,6},{3,7},{4,0},{5,1},{6,2},{7,3},{8,12},{9,13},{10,... | collective-permute-start | bytes 6291464 | tf_op jit(solution)/shard_map/ppermute | solution.py:86
  164.2 0.1 fusion.39
  164.3 0.2 reduce_window_sum.11
  164.5 0.2 select_reduce_fusion.2
  164.7 0.1 select_reduce_fusion.1
  164.8 0.7 all_to_all.12
  165.5 7.4 %all-to-all-start = ((s32[32,1,8]{2,1,0:T(1,128)}), s32[32,1,8]{2,1,0:T(1,128)S(1)}, u32[]{:S(2)}, u32[]{:S(2)}) async-start(s32[32,1,8]{2,1,0:T(1,128)} %bitcast.6), calls=%async_computation | async-start | bytes 32768 | tf_op jit(solution)/shard_map/all_to_all | solution.py:89
  172.9 0.0 copy-start.4
  172.9 1.1 fusion.4
  174.0 2.5 all-to-all-done
  176.5 7.6 %all-to-all-start.1 = ((bf16[32,8,1024]{2,1,0:T(8,128)(2,1)}), bf16[32,8,1024]{2,1,0:T(8,128)(2,1)S(1)}, u32[]{:S(2)}, u32[]{:S(2)}) async-start(bf16[32,8,1024]{2,1,0:T(8,128)(2,1)} %fusion.4), calls=%async_computation.1 | async-start | bytes 1048576 | tf_op jit(solution)/shard_map/all_to_all | solution.py:88
  184.2 0.1 sub.34
  184.3 7.9 %all-to-all-done.1 = bf16[32,8,1024]{2,1,0:T(8,128)(2,1)S(1)} async-done(((bf16[32,8,1024]{2,1,0:T(8,128)(2,1)}), bf16[32,8,1024]{2,1,0:T(8,128)(2,1)S(1)}, u32[]{:S(2)}, u32[]{:S(2)}) %all-to-all-start.1) | async-done | bytes 524320 | tf_op jit(solution)/shard_map/all_to_all | solution.py:88
  192.2 0.0 copy-done
  192.2 0.3 fusion.20
  192.5 84.8 %all-reduce.1 = bf16[256,128]{0,1:T(8,128)(2,1)S(1)} all-reduce(f32[256,128]{0,1:T(8,128)S(1)} %bitcast.80), channel_id=1, replica_groups=mesh['dp'=32,'mp'=8] {'mp'}, use_global_device_ids=true, to_apply=%region_6.7 | all-reduce | flops 32768 | bytes 196608 | tf_op jit(solution)/shard_map/psum | solution.py:97
  277.3 0.0 copy-done.1
  277.3 1.0 fusion.19
  278.3 7.4 %all-to-all-start.2 = ((bf16[32,8,512]{2,1,0:T(8,128)(2,1)}), bf16[32,8,512]{2,1,0:T(8,128)(2,1)S(1)}, u32[]{:S(2)}, u32[]{:S(2)}) async-start(bf16[32,8,512]{2,1,0:T(8,128)(2,1)} %fusion.19), calls=%async_computation.2 | async-start | bytes 524288 | tf_op jit(solution)/shard_map/all_to_all | solution.py:103
  285.7 0.0 copy-done.4
  285.7 5.3 %all-to-all-done.2 = bf16[32,8,512]{2,1,0:T(8,128)(2,1)S(1)} async-done(((bf16[32,8,512]{2,1,0:T(8,128)(2,1)}), bf16[32,8,512]{2,1,0:T(8,128)(2,1)S(1)}, u32[]{:S(2)}, u32[]{:S(2)}) %all-to-all-start.2) | async-done | bytes 262176 | tf_op jit(solution)/shard_map/all_to_all | solution.py:103
  291.0 0.0 collective-permute-done.2
  291.0 1.8 fusion.28
  (10 shorter events, 0.2 us)
Async XLA Ops:
  0.0 192.2 %copy-start = (bf16[2,1024,64]{1,2,0:T(8,128)(2,1)S(1)}, bf16[2,1024,64]{1,2,0:T(8,128)(2,1)}, u32[]{:S(2)}) copy-start(bf16[2,1024,64]{1,2,0:T(8,128)(2,1)} %param.22) | copy-start | bytes 786436
  16.5 51.3 %copy-start.2 = (s32[4096]{0:T(1024)S(1)}, s32[4096]{0:T(1024)}, u32[]{:S(2)}) copy-start(s32[4096]{0:T(1024)} %param.20) | copy-start | bytes 49156
  16.5 51.3 %copy-start.3 = (s32[128]{0:T(128)S(1)}, s32[128]{0:T(128)}, u32[]{:S(2)}) copy-start(s32[128]{0:T(128)} %param.19) | copy-start | bytes 1540
  16.5 47.6 %collective-permute-start = (f32[128,4096]{1,0:T(8,128)S(1)}, f32[128,4096]{1,0:T(8,128)S(1)}, u32[]{:S(2)}, u32[]{:S(2)}) collective-permute-start(f32[128,4096]{1,0:T(8,128)S(1)} %fusion.24), channel_id=1, source_target_pairs={{0,1},{1,0},{2,3},{3,2},{4,5},{5,4},{6,7},{7,6},{8,9},{9,8},{10,11... | collective-permute-start | bytes 6291464 | tf_op jit(solution)/shard_map/ppermute | solution.py:86
  64.5 93.3 %collective-permute-start.1 = (f32[128,4096]{1,0:T(8,128)S(1)}, f32[128,4096]{1,0:T(8,128)S(1)}, u32[]{:S(2)}, u32[]{:S(2)}) collective-permute-start(f32[128,4096]{1,0:T(8,128)S(1)} %add.74), channel_id=1, source_target_pairs={{0,2},{1,3},{2,0},{3,1},{4,6},{5,7},{6,4},{7,5},{8,10},{9,11},{10,... | collective-permute-start | bytes 6291464 | tf_op jit(solution)/shard_map/ppermute | solution.py:86
  158.0 119.4 %copy-start.1 = (bf16[2,64,512]{2,1,0:T(8,128)(2,1)S(1)}, bf16[2,64,512]{2,1,0:T(8,128)(2,1)}, u32[]{:S(2)}) copy-start(bf16[2,64,512]{2,1,0:T(8,128)(2,1)} %param.23) | copy-start | bytes 393220
  158.0 133.0 %collective-permute-start.2 = (f32[128,4096]{1,0:T(8,128)S(1)}, f32[128,4096]{1,0:T(8,128)}, u32[]{:S(2)}, u32[]{:S(2)}) collective-permute-start(f32[128,4096]{1,0:T(8,128)S(1)} %add.75), channel_id=1, source_target_pairs={{0,4},{1,5},{2,6},{3,7},{4,0},{5,1},{6,2},{7,3},{8,12},{9,13},{10,... | collective-permute-start | bytes 6291464 | tf_op jit(solution)/shard_map/ppermute | solution.py:86
  165.5 11.0 %all-to-all-start = ((s32[32,1,8]{2,1,0:T(1,128)}), s32[32,1,8]{2,1,0:T(1,128)S(1)}, u32[]{:S(2)}, u32[]{:S(2)}) async-start(s32[32,1,8]{2,1,0:T(1,128)} %bitcast.6), calls=%async_computation | async-start | bytes 32768 | tf_op jit(solution)/shard_map/all_to_all | solution.py:89
  172.9 112.8 %copy-start.4 = (s32[128]{0:T(128)S(1)}, s32[128]{0:T(128)}, u32[]{:S(2)}) copy-start(s32[128]{0:T(128)} %param.18) | copy-start | bytes 1540
  176.5 15.7 %all-to-all-start.1 = ((bf16[32,8,1024]{2,1,0:T(8,128)(2,1)}), bf16[32,8,1024]{2,1,0:T(8,128)(2,1)S(1)}, u32[]{:S(2)}, u32[]{:S(2)}) async-start(bf16[32,8,1024]{2,1,0:T(8,128)(2,1)} %fusion.4), calls=%async_computation.1 | async-start | bytes 1048576 | tf_op jit(solution)/shard_map/all_to_all | solution.py:88
  278.3 12.7 %all-to-all-start.2 = ((bf16[32,8,512]{2,1,0:T(8,128)(2,1)}), bf16[32,8,512]{2,1,0:T(8,128)(2,1)S(1)}, u32[]{:S(2)}, u32[]{:S(2)}) async-start(bf16[32,8,512]{2,1,0:T(8,128)(2,1)} %fusion.19), calls=%async_computation.2 | async-start | bytes 524288 | tf_op jit(solution)/shard_map/all_to_all | solution.py:103
